TPU v7x, 256 devices: a whole 4x4x8 slice. The times are simulated.
256 devices in a mesh: row: 16 (over y_lo, x, core), col: 16 (over y_hi, z).
Axes of the slice: x: 4, y: 4 (y_hi: 2, y_lo: 2; y = y_hi * 2 + y_lo), z: 8, core: 2. Of those that a mesh axis runs over, the one named last changes fastest.
Arguments:
- tokens: bfloat16 [512, 12288], P('row', 'col'), may hold values from -6 to 6
- out_grad: bfloat16 [512, 12288], P('row', 'col'), may hold values from -6 to 6
- w_in: bfloat16 [12288, 24576], P('col', 'row'), may hold values from -0.0546875 to 0.0546875
- w_out: bfloat16 [24576, 12288], P('row', 'col'), may hold values from -0.0390625 to 0.0390625
- bias_in: float32 [24576], P('row'), may hold values from -3 to 3
- stream_ids: int32 [3], replicated, may hold values from 0 to 4095
- tile_keys: int32 [64, 192], replicated, may hold values from 0 to 16777215
Outputs:
- grad_tokens: bfloat16 [512, 12288], P('row', 'col')
- grad_w_in: bfloat16 [12288, 24576], P('col', 'row')
- grad_w_out: bfloat16 [24576, 12288], P('row', 'col')
- grad_bias_in: float32 [24576], P('row')
- grad_bias_out: float32 [12288], P('col')
All inputs are finite; a program needn't handle non-finite values.
Results may differ from a plain program's by a relative error of at most 0.005.
Values may be sent and summed in bfloat16 or wider, within the bound.
No kernel may reach another device: no remote copies, remote signals or barrier semaphores. Data moves between devices by JAX's collectives and lax.ppermute only.
A program may use at most 64 MiB of HBM per device.

v0:
```python
import jax
import jax.numpy as jnp
from jax import lax
from jax.sharding import PartitionSpec as P

TILE_T = 8
TILE_F = 128
mix_one = 73856093
mix_two = 19349663
mix_three = 83492791
golden = -1640531535
mult_one = 2146121005
mult_two = -2073254261


def shift_down(value, count):
    return lax.shift_right_logical(value, jnp.full(value.shape, count, jnp.int32))


def keep_mask(tile_keys, stream_ids, row_start, row_count, col_start, col_count, tile_t, tile_f):
    row_ids = row_start + jnp.arange(row_count, dtype=jnp.int32)
    col_ids = col_start + jnp.arange(col_count, dtype=jnp.int32)
    onehot_rows = (
        row_ids[:, None] // tile_t == jnp.arange(tile_keys.shape[0], dtype=jnp.int32)[None, :]
    ).astype(jnp.int32)
    onehot_cols = (
        jnp.arange(tile_keys.shape[1], dtype=jnp.int32)[:, None] == col_ids[None, :] // tile_f
    ).astype(jnp.int32)
    picked = jnp.dot(onehot_rows, tile_keys, preferred_element_type=jnp.int32)
    picked = jnp.dot(picked, onehot_cols, preferred_element_type=jnp.int32)
    salt = (
        stream_ids[0] * jnp.int32(mix_one)
        ^ stream_ids[1] * jnp.int32(mix_two)
        ^ stream_ids[2] * jnp.int32(mix_three)
    )
    offset = row_ids[:, None] % tile_t * tile_f + col_ids[None, :] % tile_f
    value = (picked ^ salt) + offset * jnp.int32(golden)
    value = value ^ shift_down(value, 16)
    value = value * jnp.int32(mult_one)
    value = value ^ shift_down(value, 15)
    value = value * jnp.int32(mult_two)
    value = value ^ shift_down(value, 16)
    return (shift_down(value, 8) & jnp.int32(1023) < jnp.int32(922)).astype(jnp.float32)


def normal_cdf(value):
    return 0.5 * (1.0 + lax.erf(value * 0.7071067811865476))


def local_gelu(pre_part, dact_part, bias_part, keep):
    pre = pre_part + bias_part
    scaled = keep * (1.0 / 0.9)
    cdf = normal_cdf(pre)
    act = (pre * cdf * scaled).astype(jnp.bfloat16)
    slope = cdf + pre * jnp.exp(-0.5 * pre * pre) * 0.3989422804014327
    dpre = (dact_part * scaled * slope).astype(jnp.bfloat16)
    return (act, dpre)


def local(tokens, out_grad, w_in, w_out, bias_in, stream_ids, tile_keys):
    col_count = lax.axis_size("col")
    row_index = lax.axis_index("row")
    col_index = lax.axis_index("col")
    ff_local = w_in.shape[1]
    all_tokens, all_grads = (
        lax.all_gather(tokens, "row", axis=0, tiled=True),
        lax.all_gather(out_grad, "row", axis=0, tiled=True),
    )
    total_tokens = all_tokens.shape[0]
    pre_terms = jnp.dot(all_tokens, w_in, preferred_element_type=jnp.float32)
    dact_terms = lax.dot_general(
        all_grads, w_out, (((1,), (1,)), ((), ())), preferred_element_type=jnp.float32
    )
    pre_part, dact_part = (
        lax.psum_scatter(pre_terms, "col", scatter_dimension=0, tiled=True),
        lax.psum_scatter(dact_terms, "col", scatter_dimension=0, tiled=True),
    )
    height = total_tokens // col_count
    keep = keep_mask(
        tile_keys,
        stream_ids,
        col_index * height,
        height,
        row_index * ff_local,
        ff_local,
        TILE_T,
        TILE_F,
    )
    act, dpre = local_gelu(pre_part, dact_part, bias_in[None, :], keep)
    act_all, dpre_all = (
        lax.all_gather(act, "col", axis=0, tiled=True),
        lax.all_gather(dpre, "col", axis=0, tiled=True),
    )
    grad_w_out = lax.dot_general(
        act_all, all_grads, (((0,), (0,)), ((), ())), preferred_element_type=jnp.float32
    ).astype(jnp.bfloat16)
    grad_w_in = lax.dot_general(
        all_tokens, dpre_all, (((0,), (0,)), ((), ())), preferred_element_type=jnp.float32
    ).astype(jnp.bfloat16)
    grad_tokens = lax.psum_scatter(
        lax.dot_general(
            dpre_all, w_in, (((1,), (1,)), ((), ())), preferred_element_type=jnp.float32
        ),
        "row",
        scatter_dimension=0,
        tiled=True,
    ).astype(jnp.bfloat16)
    grad_bias_in = jnp.sum(dpre_all.astype(jnp.float32), axis=0)
    grad_bias_out = jnp.sum(all_grads.astype(jnp.float32), axis=0)
    return (grad_tokens, grad_w_in, grad_w_out, grad_bias_in, grad_bias_out)


def solution(mesh):
    return jax.shard_map(
        local,
        mesh=mesh,
        in_specs=(
            P("row", "col"),
            P("row", "col"),
            P("col", "row"),
            P("row", "col"),
            P("row"),
            P(),
            P(),
        ),
        out_specs=(P("row", "col"), P("col", "row"), P("row", "col"), P("row"), P("col")),
        check_vma=False,
    )
```

profile of v0, /device:TPU:32, one launch (start us, length us, event | category | flops | bytes accessed | tf_op | source)
XLA Modules:
  0.0 694.8 jit_solution(11404582454193071969)
XLA Ops:
  7.2 0.0 copy-start
  7.2 0.0 reduce-scatter.6.cloned.1.call-start
  7.2 22.2 %all_gather.13 = bf16[512,768]{1,0:T(8,128)(2,1)S(1)} all-gather(bf16[32,768]{1,0:T(8,128)(2,1)} %param.7), channel_id=1, replica_groups=mesh['row'=16,'col'=16] {'row'}, dimensions={0}, use_global_device_ids=true | all-gather | bytes 835584 | tf_op jit(solution)/shard_map/all_gather | solution.py:66
  29.4 0.0 copy-done
  29.5 0.0 copy-start.1
  29.5 3.0 fusion.45
  32.5 0.0 copy-done.1
  32.5 0.0 copy-start.2
  32.5 0.0 reduce-scatter.6.cloned.1.call-update
  32.5 0.0 reduce-scatter.4.cloned.1.call-start
  32.6 0.7 copy-done.2
  33.3 18.4 %all_gather.12 = bf16[512,768]{1,0:T(8,128)(2,1)S(1)} all-gather(bf16[32,768]{1,0:T(8,128)(2,1)S(1)} %copy-done.2), channel_id=1, replica_groups=mesh['row'=16,'col'=16] {'row'}, dimensions={0}, use_global_device_ids=true | all-gather | bytes 835584 | tf_op jit(solution)/shard_map/all_gather | solution.py:67
  51.7 4.8 fusion.44
  56.5 0.0 copy-start.3
  56.5 0.0 copy-start.4
  56.5 0.0 copy-start.5
  56.5 0.0 reduce-scatter.4.cloned.1.call-update
  56.5 0.0 all-gather.3.cloned.1.call-start
  56.5 0.6 copy-done.3
  57.1 0.6 fusion.43
  59.7 183.7 %reduce-scatter.6.cloned.1.call-done = f32[32,1536]{1,0:T(8,128)} async-done(((f32[512,1536]{1,0:T(8,128)}), f32[32,1536]{1,0:T(8,128)}) %reduce-scatter.6.cloned.1.call-update) | async-done | bytes 196624 | tf_op jit(solution)/shard_map/reduce_scatter | solution.py:75
  243.4 213.6 %reduce-scatter.4.cloned.1.call-done = f32[32,1536]{1,0:T(8,128)} async-done(((f32[512,1536]{1,0:T(8,128)}), f32[32,1536]{1,0:T(8,128)}) %reduce-scatter.4.cloned.1.call-update) | async-done | bytes 196624 | tf_op jit(solution)/shard_map/reduce_scatter | solution.py:76
  457.0 0.0 copy-done.4
  457.0 0.0 copy-done.5
  457.0 2.6 multiply_convert_fusion
  459.6 0.0 all-gather.3.cloned.1.call-update
  459.6 0.0 all-gather.5.cloned.1.call-start
  459.7 0.5 all-gather.5.cloned.1.call-update
  460.2 0.0 reduce-scatter.8.cloned.1.call-start
  460.2 80.2 %all-gather.3.cloned.1.call-done = bf16[512,1536]{1,0:T(8,128)(2,1)} async-done(((bf16[32,1536]{1,0:T(8,128)(2,1)}), bf16[512,1536]{1,0:T(8,128)(2,1)}) %all-gather.3.cloned.1.call-update) | async-done | bytes 1572880 | tf_op jit(solution)/shard_map/all_gather | solution.py:92
  540.5 4.0 fusion.46
  544.4 0.0 reduce-scatter.8.cloned.1.call-update
  544.5 0.7 convert_reduce_fusion.1
  545.2 4.4 fusion
  549.6 4.3 copy.12
  553.9 2.3 convert_reduce_fusion
  556.2 65.3 %all-gather.5.cloned.1.call-done = bf16[512,1536]{1,0:T(8,128)(2,1)} async-done(((bf16[32,1536]{1,0:T(8,128)(2,1)}), bf16[512,1536]{1,0:T(8,128)(2,1)}) %all-gather.5.cloned.1.call-update) | async-done | bytes 1572880 | tf_op jit(solution)/shard_map/all_gather | solution.py:91
  621.5 4.2 convolution_convert_fusion
  625.7 61.0 %reduce-scatter.8.cloned.1.call-done = f32[32,768]{1,0:T(8,128)} async-done(((f32[512,768]{1,0:T(8,128)}), f32[32,768]{1,0:T(8,128)}) %reduce-scatter.8.cloned.1.call-update) | async-done | bytes 98320 | tf_op jit(solution)/shard_map/reduce_scatter | solution.py:100
  686.7 1.5 convert_element_type.28
  (2 shorter events, 0.0 us)
Async XLA Ops:
  7.2 22.3 %copy-start = (bf16[768,1536]{1,0:T(8,128)(2,1)S(1)}, bf16[768,1536]{1,0:T(8,128)(2,1)}, u32[]{:S(2)}) copy-start(bf16[768,1536]{1,0:T(8,128)(2,1)} %param.9) | copy-start | bytes 7077892
  7.2 236.2 %reduce-scatter.6.cloned.1.call-start = ((), (), s32[]{:S(2)}) async-start(), calls=%async_computation.4 | async-start | bytes 3342336 | tf_op jit(solution)/shard_map/reduce_scatter | solution.py:75
  29.5 3.0 copy-start.1
  32.5 0.8 copy-start.2
  32.5 424.5 %reduce-scatter.4.cloned.1.call-start = ((), (), s32[]{:S(2)}) async-start(), calls=%async_computation.3 | async-start | bytes 3342336 | tf_op jit(solution)/shard_map/reduce_scatter | solution.py:76
  56.5 0.7 copy-start.3
  56.5 400.5 %copy-start.4 = (s32[64,192]{1,0:T(8,128)S(1)}, s32[64,192]{1,0:T(8,128)}, u32[]{:S(2)}) copy-start(s32[64,192]{1,0:T(8,128)} %param.13) | copy-start | bytes 147460
  56.5 400.5 %copy-start.5 = (f32[1536]{0:T(1024)S(1)}, f32[1536]{0:T(1024)}, u32[]{:S(2)}) copy-start(f32[1536]{0:T(1024)} %param.11) | copy-start | bytes 18436
  56.5 484.0 %all-gather.3.cloned.1.call-start = ((), (), s32[]{:S(2)}) async-start(), calls=%async_computation.5 | async-start | bytes 1671168 | tf_op jit(solution)/shard_map/all_gather | solution.py:92
  459.6 161.9 %all-gather.5.cloned.1.call-start = ((), (), s32[]{:S(2)}) async-start(), calls=%async_computation.7 | async-start | bytes 1671168 | tf_op jit(solution)/shard_map/all_gather | solution.py:91
  460.2 226.6 %reduce-scatter.8.cloned.1.call-start = ((), (), s32[]{:S(2)}) async-start(), calls=%async_computation.6 | async-start | bytes 1671168 | tf_op jit(solution)/shard_map/reduce_scatter | solution.py:100
Sparse Core Ops, SparseCore 0:
  32.6 210.7 reduce-scatter.5
  247.4 209.5 reduce-scatter.3
  460.2 80.2 all-gather.2
  542.9 78.5 all-gather.4
  623.9 62.8 reduce-scatter.7
where the time goes:
time: 695 us
  waiting for transfers between devices  604 us (87%)
  blocking collectives  40.6 us (6%)
  matrix products  23 us (3%)
  between operations  15.8 us (2%)
    reduce_scatter x1, waiting for transfers between devices, local(): lax.psum_scatter(dact_terms, 'col', scatter_dimension=0, tiled=True)  214 us
    reduce_scatter x1, waiting for transfers between devices, local(): lax.psum_scatter(pre_terms, 'col', scatter_dimension=0, tiled=True)  184 us
    all_gather x1, waiting for transfers between devices, local(): lax.all_gather(dpre, 'col', axis=0, tiled=True)  80.2 us
    all_gather x1, waiting for transfers between devices, local(): lax.all_gather(act, 'col', axis=0, tiled=True)  65.3 us
    reduce_scatter x1, waiting for transfers between devices, local(): lax.psum_scatter(lax.dot_general(dpre_all, w_in, (((1,), (1,)), ((), ()))...  61 us
    all_gather x1, blocking collectives, local(): lax.all_gather(tokens, 'row', axis=0, tiled=True)  22.2 us
    all_gather x1, blocking collectives, local(): lax.all_gather(out_grad, 'row', axis=0, tiled=True)  18.4 us
  transfers between devices with their start and end apart: 5, of which 5 were waited for; matrix products, arithmetic and copies ran while one was open for 4% of the time, Pallas kernels for 0%

commit v1 on v0

--- a/solution.py
+++ b/solution.py
@@ -89,7 +89,9 @@
     act, dpre = local_gelu(pre_part, dact_part, bias_in[None, :], keep)
     act_all, dpre_all = (
         lax.all_gather(act, "col", axis=0, tiled=True),
-        lax.all_gather(dpre, "col", axis=0, tiled=True),
+        jnp.concatenate(
+            lax.all_to_all(jnp.stack([dpre] * lax.axis_size("col")), "col", 0, 0), axis=0
+        ),
     )
     grad_w_out = lax.dot_general(
         act_all, all_grads, (((0,), (0,)), ((), ())), preferred_element_type=jnp.float32

time: 695 us -> 630 us (0.906)
  waiting for transfers between devices: 604 us -> 530 us
    all_gather x1 -> x0, waiting for transfers between devices: 80.2 us -> none  [local(): lax.all_gather(dpre, 'col', axis=0, tiled=True)]
    all_to_all x0 -> x1, waiting for transfers between devices: none -> 36.2 us  [local(): lax.all_to_all(jnp.stack([dpre] * lax.axis_size('col')), 'col', 0, 0)]
    all_gather x1, waiting for transfers between devices: 65.3 us -> 35.2 us  [local(): lax.all_gather(act, 'col', axis=0, tiled=True)]
where the time goes in v1:
time: 630 us; the launch traced here: 629 us
  waiting for transfers between devices  530 us (84%)
  blocking collectives  40.6 us (6%)
  matrix products  23 us (4%)
  between operations  15.8 us (3%)
  local copies, waits for them, and re-layouts  7.51 us (1%)
  starting transfers between devices  7.03 us (1%)
    reduce_scatter x1, waiting for transfers between devices, local(): lax.psum_scatter(dact_terms, 'col', scatter_dimension=0, tiled=True)  214 us
    reduce_scatter x1, waiting for transfers between devices, local(): lax.psum_scatter(pre_terms, 'col', scatter_dimension=0, tiled=True)  184 us
    reduce_scatter x1, waiting for transfers between devices, local(): lax.psum_scatter(lax.dot_general(dpre_all, w_in, (((1,), (1,)), ((), ()))...  61 us
    all_to_all x1, waiting for transfers between devices, local(): lax.all_to_all(jnp.stack([dpre] * lax.axis_size('col')), 'col', 0, 0)  36.2 us
    all_gather x1, waiting for transfers between devices, local(): lax.all_gather(act, 'col', axis=0, tiled=True)  35.2 us
    all_gather x1, blocking collectives, local(): lax.all_gather(tokens, 'row', axis=0, tiled=True)  22.2 us
    all_gather x1, blocking collectives, local(): lax.all_gather(out_grad, 'row', axis=0, tiled=True)  18.4 us
  transfers between devices with their start and end apart: 5, of which 5 were waited for; matrix products, arithmetic and copies ran while one was open for 4% of the time, Pallas kernels for 0%

profile of v1, /device:TPU:32, one launch (start us, length us, event | category | flops | bytes accessed | tf_op | source)
XLA Modules:
  0.0 628.9 jit_solution(4961322047628718233)
XLA Ops:
  7.2 0.0 copy-start
  7.2 0.0 reduce-scatter.6.cloned.1.call-start
  7.2 22.2 %all_gather.10 = bf16[512,768]{1,0:T(8,128)(2,1)S(1)} all-gather(bf16[32,768]{1,0:T(8,128)(2,1)} %param.7), channel_id=1, replica_groups=mesh['row'=16,'col'=16] {'row'}, dimensions={0}, use_global_device_ids=true | all-gather | bytes 835584 | tf_op jit(solution)/shard_map/all_gather | solution.py:66
  29.4 0.0 copy-done
  29.5 0.0 copy-start.1
  29.5 3.0 fusion.45
  32.5 0.0 copy-done.1
  32.5 0.0 copy-start.2
  32.5 0.0 reduce-scatter.6.cloned.1.call-update
  32.5 0.0 reduce-scatter.4.cloned.1.call-start
  32.6 0.7 copy-done.2
  33.3 18.4 %all_gather.9 = bf16[512,768]{1,0:T(8,128)(2,1)S(1)} all-gather(bf16[32,768]{1,0:T(8,128)(2,1)S(1)} %copy-done.2), channel_id=1, replica_groups=mesh['row'=16,'col'=16] {'row'}, dimensions={0}, use_global_device_ids=true | all-gather | bytes 835584 | tf_op jit(solution)/shard_map/all_gather | solution.py:67
  51.7 4.8 fusion.44
  56.5 0.0 copy-start.3
  56.5 0.0 copy-start.4
  56.5 0.0 copy-start.5
  56.5 0.0 reduce-scatter.4.cloned.1.call-update
  56.5 0.6 copy-done.3
  57.1 0.6 fusion.43
  59.7 183.7 %reduce-scatter.6.cloned.1.call-done = f32[32,1536]{1,0:T(8,128)} async-done(((f32[512,1536]{1,0:T(8,128)}), f32[32,1536]{1,0:T(8,128)}) %reduce-scatter.6.cloned.1.call-update) | async-done | bytes 196624 | tf_op jit(solution)/shard_map/reduce_scatter | solution.py:75
  243.4 213.6 %reduce-scatter.4.cloned.1.call-done = f32[32,1536]{1,0:T(8,128)} async-done(((f32[512,1536]{1,0:T(8,128)}), f32[32,1536]{1,0:T(8,128)}) %reduce-scatter.4.cloned.1.call-update) | async-done | bytes 196624 | tf_op jit(solution)/shard_map/reduce_scatter | solution.py:76
  457.0 0.0 copy-done.4
  457.0 0.0 copy-done.5
  457.0 2.5 multiply_convert_fusion
  459.6 1.3 stack.2
  460.9 6.9 %all-to-all-start = ((bf16[16,32,1536]{2,1,0:T(8,128)(2,1)}), bf16[16,32,1536]{2,1,0:T(8,128)(2,1)}, u32[]{:S(2)}, u32[]{:S(2)}) async-start(bf16[16,32,1536]{2,1,0:T(8,128)(2,1)} %stack.2), calls=%async_computation.2 | async-start | bytes 3145728 | tf_op jit(solution)/shard_map/all_to_all | solution.py:93
  467.7 0.0 all-gather.2.cloned.1.call-start
  467.8 0.7 all-gather.2.cloned.1.call-update
  468.5 0.0 reduce-scatter.8.cloned.1.call-start
  468.5 36.2 %all-to-all-done = bf16[16,32,1536]{2,1,0:T(8,128)(2,1)} async-done(((bf16[16,32,1536]{2,1,0:T(8,128)(2,1)}), bf16[16,32,1536]{2,1,0:T(8,128)(2,1)}, u32[]{:S(2)}, u32[]{:S(2)}) %all-to-all-start) | async-done | bytes 1572896 | tf_op jit(solution)/shard_map/all_to_all | solution.py:93
  504.8 4.0 fusion.46
  508.7 0.0 reduce-scatter.8.cloned.1.call-update
  508.7 0.7 convert_reduce_fusion.1
  509.5 4.4 fusion
  513.9 4.3 copy.13
  518.2 2.3 convert_reduce_fusion
  520.5 35.2 %all-gather.2.cloned.1.call-done = bf16[512,1536]{1,0:T(8,128)(2,1)} async-done(((bf16[32,1536]{1,0:T(8,128)(2,1)}), bf16[512,1536]{1,0:T(8,128)(2,1)}) %all-gather.2.cloned.1.call-update) | async-done | bytes 1572880 | tf_op jit(solution)/shard_map/all_gather | solution.py:91
  555.6 4.2 convolution_convert_fusion
  559.9 61.0 %reduce-scatter.8.cloned.1.call-done = f32[32,768]{1,0:T(8,128)} async-done(((f32[512,768]{1,0:T(8,128)}), f32[32,768]{1,0:T(8,128)}) %reduce-scatter.8.cloned.1.call-update) | async-done | bytes 98320 | tf_op jit(solution)/shard_map/reduce_scatter | solution.py:102
  620.9 1.5 convert_element_type.29
  (2 shorter events, 0.0 us)
Async XLA Ops:
  7.2 22.3 %copy-start = (bf16[768,1536]{1,0:T(8,128)(2,1)S(1)}, bf16[768,1536]{1,0:T(8,128)(2,1)}, u32[]{:S(2)}) copy-start(bf16[768,1536]{1,0:T(8,128)(2,1)} %param.9) | copy-start | bytes 7077892
  7.2 236.2 %reduce-scatter.6.cloned.1.call-start = ((), (), s32[]{:S(2)}) async-start(), calls=%async_computation.5 | async-start | bytes 3342336 | tf_op jit(solution)/shard_map/reduce_scatter | solution.py:75
  29.5 3.0 copy-start.1
  32.5 0.8 copy-start.2
  32.5 424.5 %reduce-scatter.4.cloned.1.call-start = ((), (), s32[]{:S(2)}) async-start(), calls=%async_computation.4 | async-start | bytes 3342336 | tf_op jit(solution)/shard_map/reduce_scatter | solution.py:76
  56.5 0.7 copy-start.3
  56.5 400.6 %copy-start.4 = (s32[64,192]{1,0:T(8,128)S(1)}, s32[64,192]{1,0:T(8,128)}, u32[]{:S(2)}) copy-start(s32[64,192]{1,0:T(8,128)} %param.13) | copy-start | bytes 147460
  56.5 400.6 %copy-start.5 = (f32[1536]{0:T(1024)S(1)}, f32[1536]{0:T(1024)}, u32[]{:S(2)}) copy-start(f32[1536]{0:T(1024)} %param.11) | copy-start | bytes 18436
  460.9 43.9 %all-to-all-start = ((bf16[16,32,1536]{2,1,0:T(8,128)(2,1)}), bf16[16,32,1536]{2,1,0:T(8,128)(2,1)}, u32[]{:S(2)}, u32[]{:S(2)}) async-start(bf16[16,32,1536]{2,1,0:T(8,128)(2,1)} %stack.2), calls=%async_computation.2 | async-start | bytes 3145728 | tf_op jit(solution)/shard_map/all_to_all | solution.py:93
  467.7 87.9 %all-gather.2.cloned.1.call-start = ((), (), s32[]{:S(2)}) async-start(), calls=%async_computation.7 | async-start | bytes 1671168 | tf_op jit(solution)/shard_map/all_gather | solution.py:91
  468.5 152.4 %reduce-scatter.8.cloned.1.call-start = ((), (), s32[]{:S(2)}) async-start(), calls=%async_computation.6 | async-start | bytes 1671168 | tf_op jit(solution)/shard_map/reduce_scatter | solution.py:102
Sparse Core Ops, SparseCore 0:
  32.6 210.7 reduce-scatter.5
  247.4 209.5 reduce-scatter.3
  471.1 84.4 all-gather.1
  558.0 62.8 reduce-scatter.7
